TPU v7x, 512 devices: a whole 4x4x16 slice. The times are simulated.
512 devices in a mesh: row: 16 (over x, z_hi, core), col: 32 (over y, z_lo).
Axes of the slice: x: 4, y: 4, z: 16 (z_hi: 2, z_lo: 8; z = z_hi * 8 + z_lo), core: 2. Of those that a mesh axis runs over, the one named last changes fastest.
Arguments:
- pair: bfloat16 [768, 768, 128], P('row', 'col'), may hold values from -6 to 6
- token_mask: int32 [768], P('col'), may hold values from 0 to 1, as said below
- w_query: bfloat16 [128, 128], replicated, may hold values from -0.5 to 0.5
- w_key: bfloat16 [128, 128], replicated, may hold values from -0.5 to 0.5
- w_value: bfloat16 [128, 128], replicated, may hold values from -0.5 to 0.5
- w_gate: bfloat16 [128, 128], replicated, may hold values from -0.5 to 0.5
- w_bias: bfloat16 [128, 4], replicated
- w_out: bfloat16 [128, 128], replicated, may hold values from -0.5 to 0.5
- w_hidden_a: bfloat16 [128, 512], replicated, may hold values from -0.5 to 0.5
- w_hidden_b: bfloat16 [128, 512], replicated, may hold values from -0.5 to 0.5
- w_hidden_out: bfloat16 [512, 128], replicated, may hold values from -0.25 to 0.25
Outputs:
- updated_rows: bfloat16 [320, 768, 128], P('row', 'col')
Inputs may be any that keep to these rules, and one draw needn't show every extreme that they name: `token_mask`: the 768 residues fall into aligned blocks of 64; in each block the first 16 to 64 residues are 1 and the rest 0.
All inputs are finite; a program needn't handle non-finite values.
Results may differ from a plain program's by a relative error of at most 0.011.
The roundings to bfloat16 on the way count: a program that leaves them out, or rounds other values in their place, can miss the bound.
Values may be sent and summed in bfloat16 or wider, within the bound.
A program may use at most 64 MiB of HBM per device.

v0:
```python
import math

import jax
import jax.numpy as jnp
from jax import lax
from jax.sharding import PartitionSpec as P

HEADS = 4
HEAD_DIM = 32
QR = 20


def broadcast(value, axis, source):
    kept = jnp.where(lax.axis_index(axis) == source, value, 0).astype(value.dtype)
    return lax.psum(kept, axis)


def normalize(values_in):
    average = jnp.mean(values_in, axis=-1, keepdims=True)
    centred = values_in - average
    variance = jnp.mean(centred * centred, axis=-1, keepdims=True)
    return centred * lax.rsqrt(variance + 1e-05)


def attend(state, queries, bias_all, key_tile, value_tile, alive_tile, offset):
    running_max, running_sum, weighted = state
    rows_q = key_tile.shape[0]
    tile_keys = key_tile.shape[1]
    keys_split = key_tile.reshape(rows_q, tile_keys, HEADS, HEAD_DIM)
    values_split = value_tile.reshape(rows_q, tile_keys, HEADS, HEAD_DIM)
    scores = jnp.einsum("ijhd,ikhd->hijk", queries, keys_split, preferred_element_type=jnp.float32)
    bias_tile = lax.dynamic_slice_in_dim(bias_all, offset, tile_keys, 2)
    scores = scores + bias_tile[:, None].astype(jnp.float32)
    alive = alive_tile[0] > 0
    masked = jnp.where(alive, scores, jnp.float32(-1e30))
    new_max = jnp.maximum(running_max, jnp.max(masked, axis=-1))
    weights = jnp.where(alive, jnp.exp(scores - new_max[..., None]), jnp.float32(0.0))
    factor = jnp.exp(running_max - new_max)
    running_sum = running_sum * factor + jnp.sum(weights, axis=-1)
    weighted = weighted * factor[..., None] + jnp.einsum(
        "hijk,ikhd->hijd",
        weights.astype(jnp.bfloat16),
        values_split,
        preferred_element_type=jnp.float32,
    )
    return (new_max, running_sum, weighted)


def local(
    pair,
    token_mask,
    w_query,
    w_key,
    w_value,
    w_gate,
    w_bias,
    w_out,
    w_hidden_a,
    w_hidden_b,
    w_hidden_out,
):
    rows_block, columns, channels = pair.shape
    normed = normalize(pair.astype(jnp.float32)).astype(jnp.bfloat16)
    bias_local = jnp.dot(
        normed.reshape(-1, channels), w_bias, preferred_element_type=jnp.float32
    ).astype(jnp.bfloat16)
    bias_local = bias_local.reshape(rows_block, columns, HEADS).transpose(2, 0, 1)
    bias_band = lax.all_gather(bias_local, "col", axis=2, tiled=True)
    column_start = lax.axis_index("col") * columns
    owner = column_start // rows_block
    bias_owned = broadcast(bias_band, "row", owner)
    bias_all = lax.dynamic_slice_in_dim(bias_owned, column_start % rows_block, columns, 1)
    window_normed = normed[:QR]
    window_flat = window_normed.reshape(-1, channels)
    score_scale = 1.0 / math.sqrt(HEAD_DIM)
    queries = (
        jnp.dot(window_flat, w_query, preferred_element_type=jnp.float32) * score_scale
    ).astype(jnp.bfloat16)
    queries = queries.reshape(QR, columns, HEADS, HEAD_DIM)
    gate_logits = jnp.dot(window_flat, w_gate, preferred_element_type=jnp.float32)
    alive_row = token_mask.astype(jnp.bfloat16)[None, :]
    start_state = (
        jnp.full((HEADS, QR, columns), -1e30, jnp.float32),
        jnp.zeros((HEADS, QR, columns), jnp.float32),
        jnp.zeros((HEADS, QR, columns, HEAD_DIM), jnp.float32),
    )
    keys_local = (
        jnp.dot(window_flat, w_key, preferred_element_type=jnp.float32)
        .astype(jnp.bfloat16)
        .reshape(QR, columns, HEADS * HEAD_DIM)
    )
    values_local = (
        jnp.dot(window_flat, w_value, preferred_element_type=jnp.float32)
        .astype(jnp.bfloat16)
        .reshape(QR, columns, HEADS * HEAD_DIM)
    )
    key_piece = lax.all_gather(keys_local, "col", axis=1, tiled=True)
    value_piece = lax.all_gather(values_local, "col", axis=1, tiled=True)
    alive_piece = lax.all_gather(alive_row, "col", axis=1, tiled=True)
    piece_width = key_piece.shape[1]
    tile_keys = math.gcd(piece_width, columns)
    tiles = piece_width // tile_keys

    def tile_step(tile_index, inner):
        begin = tile_index * tile_keys
        key_tile = lax.dynamic_slice_in_dim(key_piece, begin, tile_keys, 1)
        value_tile = lax.dynamic_slice_in_dim(value_piece, begin, tile_keys, 1)
        alive_tile = lax.dynamic_slice_in_dim(alive_piece, begin, tile_keys, 1)
        return attend(inner, queries, bias_all, key_tile, value_tile, alive_tile, begin)

    final_state = lax.fori_loop(0, tiles, tile_step, start_state)
    running_max, running_sum, weighted = final_state
    attended = weighted / running_sum[..., None]
    attended = attended.transpose(1, 2, 0, 3).reshape(QR * columns, HEADS * HEAD_DIM)
    gated = (jax.nn.sigmoid(gate_logits) * attended).astype(jnp.bfloat16)
    first = pair[:QR].reshape(-1, channels).astype(jnp.float32) + jnp.dot(
        gated, w_out, preferred_element_type=jnp.float32
    )
    normed_two = normalize(first).astype(jnp.bfloat16)
    hidden = (
        jax.nn.silu(jnp.dot(normed_two, w_hidden_a, preferred_element_type=jnp.float32))
        * jnp.dot(normed_two, w_hidden_b, preferred_element_type=jnp.float32)
    ).astype(jnp.bfloat16)
    updated = first + jnp.dot(hidden, w_hidden_out, preferred_element_type=jnp.float32)
    return updated.astype(jnp.bfloat16).reshape(QR, columns, channels)


def solution(mesh):
    return jax.shard_map(
        local,
        mesh=mesh,
        in_specs=(P("row", "col", None), P("col"), P(), P(), P(), P(), P(), P(), P(), P(), P()),
        out_specs=P("row", "col", None),
        check_vma=False,
    )
```

profile of v0, /device:TPU:6, one launch (start us, length us, event | category | flops | bytes accessed | tf_op | source)
XLA Modules:
  0.0 763.2 jit_solution(14501165268081223211)
XLA Ops:
  7.4 1.2 convert_reduce_fusion
  8.7 1.4 fusion.28
  10.1 1.3 fusion.29
  11.4 0.9 convolution_convert_fusion
  12.5 132.0 %all_gather.14 = bf16[4,48,768]{1,0,2:T(4,128)(2,1)S(1)} all-gather(bf16[4,48,24]{1,0,2:T(4,128)(2,1)S(1)} %copy.24), channel_id=1, replica_groups=mesh['row'=16,'col'=32] {'col'}, dimensions={2}, use_global_device_ids=true | all-gather | bytes 304128 | tf_op jit(solution)/shard_map/all_gather | solution.py:68
  144.5 1.3 broadcast_select_fusion
  148.2 1.3 dynamic-slice
  150.4 114.5 %all-reduce = bf16[768]{0:T(1024)(128)(2,1)S(1)} all-reduce(bf16[768]{0:T(1024)(128)(2,1)S(1)} %dynamic-update-slice), channel_id=2, replica_groups=mesh['row'=16,'col'=32] {'col'}, use_global_device_ids=true, to_apply=%add | all-reduce | flops 768 | bytes 3072
  264.9 138.9 %all-reduce.3.cloned.1.call-done = bf16[4,48,768]{1,0,2:T(4,128)(2,1)} async-done(((bf16[4,48,768]{1,0,2:T(4,128)(2,1)}), bf16[4,48,768]{1,0,2:T(4,128)(2,1)}) %all-reduce.3.cloned.1.call-update) | async-done | bytes 294928 | tf_op jit(solution)/shard_map/psum | solution.py:15
  403.8 2.6 constant_dynamic-slice_fusion.4
  406.4 216.3 %all-gather.6.cloned.1.call-done = bf16[20,768,128]{2,1,0:T(8,128)(2,1)} async-done(((bf16[20,24,128]{2,1,0:T(8,128)(2,1)}), bf16[20,768,128]{2,1,0:T(8,128)(2,1)}) %all-gather.6.cloned.1.call-update) | async-done | bytes 3932176 | tf_op jit(solution)/shard_map/all_gather | solution.py:98
  622.7 128.5 %while.18 = (s32[]{:T(128)}, f32[4,20,24]{2,1,0:T(8,128)S(1)}, f32[4,20,24]{2,1,0:T(8,128)S(1)}, f32[4,20,24,32]{3,2,1,0:T(8,128)S(1)}, bf16[1,768]{1,0:T(2,128)...) while((s32[]{:T(128)}, f32[4,20,24]{2,1,0:T(8,128)S(1)}, ...), condition=%wide.region_6.7_spmd.clone, body=%wide.region_3.6_spmd.clone.sunk | while | flops 6509263 | bytes 2551635 | solution.py:111
  622.7 1.0 constant_dynamic-slice_fusion.8
  625.8 0.8 convolution_add_fusion.3
  626.7 1.0 constant_dynamic-slice_fusion.8
  630.7 1.0 constant_dynamic-slice_fusion.8
  633.9 0.8 convolution_add_fusion.3
  634.8 1.0 constant_dynamic-slice_fusion.8
  637.9 0.8 convolution_add_fusion.3
  638.8 1.0 constant_dynamic-slice_fusion.8
  642.8 1.0 constant_dynamic-slice_fusion.8
  646.8 1.0 constant_dynamic-slice_fusion.8
  649.9 0.8 convolution_add_fusion.3
  650.8 1.0 constant_dynamic-slice_fusion.8
  654.0 0.8 convolution_add_fusion.3
  654.8 1.0 constant_dynamic-slice_fusion.8
  658.0 0.8 convolution_add_fusion.3
  658.9 1.0 constant_dynamic-slice_fusion.8
  662.0 0.8 convolution_add_fusion.3
  662.9 1.0 constant_dynamic-slice_fusion.8
  666.0 0.8 convolution_add_fusion.3
  666.9 1.0 constant_dynamic-slice_fusion.8
  670.0 0.8 convolution_add_fusion.3
  670.9 1.0 constant_dynamic-slice_fusion.8
  674.0 0.8 convolution_add_fusion.3
  674.9 1.0 constant_dynamic-slice_fusion.8
  678.9 1.0 constant_dynamic-slice_fusion.8
  683.0 1.0 constant_dynamic-slice_fusion.8
  687.0 1.0 constant_dynamic-slice_fusion.8
  690.1 0.8 convolution_add_fusion.3
  691.0 1.0 constant_dynamic-slice_fusion.8
  694.1 0.8 convolution_add_fusion.3
  695.0 1.0 constant_dynamic-slice_fusion.8
  698.1 0.8 convolution_add_fusion.3
  699.0 1.0 constant_dynamic-slice_fusion.8
  702.2 0.8 convolution_add_fusion.3
  703.0 1.0 constant_dynamic-slice_fusion.8
  706.2 0.8 convolution_add_fusion.3
  707.1 1.0 constant_dynamic-slice_fusion.8
  710.2 0.8 convolution_add_fusion.3
  711.1 1.0 constant_dynamic-slice_fusion.8
  714.2 0.8 convolution_add_fusion.3
  715.1 1.0 constant_dynamic-slice_fusion.8
  719.1 1.0 constant_dynamic-slice_fusion.8
  723.1 1.0 constant_dynamic-slice_fusion.8
  726.3 0.8 convolution_add_fusion.3
  727.1 1.0 constant_dynamic-slice_fusion.8
  731.2 1.0 constant_dynamic-slice_fusion.8
  735.2 1.0 constant_dynamic-slice_fusion.8
  739.2 1.0 constant_dynamic-slice_fusion.8
  743.2 1.0 constant_dynamic-slice_fusion.8
  747.2 1.0 constant_dynamic-slice_fusion.8
  752.7 1.2 fusion.41
  754.5 1.2 fusion.20
  (383 shorter events, 83.2 us)
Async XLA Ops:
  7.4 746.8 %copy-start = (bf16[128,512]{1,0:T(8,128)(2,1)S(1)}, bf16[128,512]{1,0:T(8,128)(2,1)}, u32[]{:S(2)}) copy-start(bf16[128,512]{1,0:T(8,128)(2,1)} %param.21) | copy-start | bytes 393220
  7.4 138.5 %copy-start.1 = (bf16[128,128]{1,0:T(8,128)(2,1)S(1)}, bf16[128,128]{1,0:T(8,128)(2,1)}, u32[]{:S(2)}) copy-start(bf16[128,128]{1,0:T(8,128)(2,1)} %param.16) | copy-start | bytes 98308
  7.4 139.4 %copy-start.2 = (bf16[128,128]{1,0:T(8,128)(2,1)S(1)}, bf16[128,128]{1,0:T(8,128)(2,1)}, u32[]{:S(2)}) copy-start(bf16[128,128]{1,0:T(8,128)(2,1)} %param.17) | copy-start | bytes 98308
  7.4 140.3 %copy-start.3 = (bf16[128,128]{1,0:T(8,128)(2,1)S(1)}, bf16[128,128]{1,0:T(8,128)(2,1)}, u32[]{:S(2)}) copy-start(bf16[128,128]{1,0:T(8,128)(2,1)} %param.15) | copy-start | bytes 98308
  7.4 396.5 %all-reduce.3.cloned.1.call-start = ((), (), s32[]{:S(2)}) async-start(), calls=%async_computation.1 | async-start | bytes 1572864 | tf_op jit(solution)/shard_map/psum | solution.py:15
  8.7 139.6 %copy-start.7 = (s32[24]{0:T(128)S(1)}, s32[24]{0:T(128)}, u32[]{:S(2)}) copy-start(s32[24]{0:T(128)} %param.14) | copy-start | bytes 292
  145.8 260.6 %all-gather.4.cloned.1.call-start = ((), (), s32[]{:S(2)}) async-start(), calls=%async_computation | async-start | bytes 4055040 | tf_op jit(solution)/shard_map/all_gather | solution.py:97
  146.8 476.0 %all-gather.6.cloned.1.call-start = ((), (), s32[]{:S(2)}) async-start(), calls=%async_computation.2 | async-start | bytes 4055040 | tf_op jit(solution)/shard_map/all_gather | solution.py:98
  751.2 1.5 slice-start
  751.2 1.5 copy-start.6
  751.3 3.3 copy-start.4
  751.6 2.9 copy-start.5
Sparse Core Ops, SparseCore 0:
  145.9 257.8 all-reduce.2
Sparse Core Ops, SparseCore 1:
  148.4 239.1 all-gather.3
  389.8 232.9 all-gather.5
where the time goes:
time: 766 us; the launch traced here: 763 us
  waiting for transfers between devices  355 us (46%)
  blocking collectives  247 us (32%)
  local copies, waits for them, and re-layouts  76.5 us (10%)
  matrix products  45.5 us (6%)
  other arithmetic  20.5 us (3%)
  between operations  15.8 us (2%)
    all_gather x1, waiting for transfers between devices, local(): value_piece = lax.all_gather(values_local, 'col', axis=1, tiled=True)  216 us
    psum x1, waiting for transfers between devices, broadcast(): return lax.psum(kept, axis)  139 us
    all_gather x1, blocking collectives, local(): bias_band = lax.all_gather(bias_local, 'col', axis=2, tiled=True)  132 us
    unnamed x1, blocking collectives  115 us
    dynamic_slice x32, local copies, waits for them, and re-layouts, tile_step(): value_tile = lax.dynamic_slice_in_dim(value_piece, begin, tile_keys, 1)  32 us
    dot_general x32, matrix products, attend(): jnp.einsum('hijk,ikhd->hijd', weights.astype(jnp.bfloat16), values_split,...  26.8 us
    dynamic_slice x32, local copies, waits for them, and re-layouts, attend(): bias_tile = lax.dynamic_slice_in_dim(bias_all, offset, tile_keys, 2)  23.9 us
  transfers between devices with their start and end apart: 3, of which 2 were waited for; matrix products, arithmetic and copies ran while one was open for 1% of the time, Pallas kernels for 0%

commit v1 on v0

v1 whole, which is shorter than its diff:
```python
import functools
import math

import jax
import jax.numpy as jnp
from jax import lax
from jax.experimental import pallas as pl
from jax.experimental.pallas import tpu as pltpu
from jax.sharding import PartitionSpec as P

HEADS = 4
HEAD_DIM = 32
QR = 20
NZ = 8
NY = 4
DEAD = -1e30
MESH = pl.DeviceIdType.MESH
F32 = jnp.float32
BF16 = jnp.bfloat16


def normalize(values_in):
    average = jnp.mean(values_in, axis=-1, keepdims=True)
    centred = values_in - average
    variance = jnp.mean(centred * centred, axis=-1, keepdims=True)
    return centred * lax.rsqrt(variance + 1e-05)


def dot(a, b):
    return jnp.dot(a, b, preferred_element_type=F32)


def dot_t(a, b):
    return lax.dot_general(a, b, (((1,), (1,)), ((), ())), preferred_element_type=F32)


def sigmoid(v):
    return 1.0 / (1.0 + jnp.exp(-v))


def kernel(
    columns,
    pair_ref,
    mask_ref,
    wq_ref,
    wk_ref,
    wv_ref,
    wg_ref,
    wb_ref,
    wo_ref,
    wha_ref,
    whb_ref,
    who_ref,
    out_ref,
    gath,
    part,
    biasg,
    bias_t,
    qk_ref,
    m_ref,
    l_ref,
    acc_ref,
    b_own,
    send_g,
    recv_g,
    send_b1,
    recv_b1,
    send_b2,
    recv_b2,
):
    rows_block = pair_ref.shape[0]
    channels = pair_ref.shape[2]
    tokens = QR * columns
    hq = HEADS * columns
    row = lax.axis_index("row")
    col = lax.axis_index("col")
    y = col // NZ
    z = col % NZ
    yp = (y + 1) % NY
    ym = (y + NY - 1) % NY
    y2 = (y + 2) % NY
    core = row % 2
    grp = row // 2
    my_q = (col % 2) * 2 + core

    def b1_dest(g):
        return 2 * g + col % 2, 2 * row + (col // 2) % 2

    def b1_source(n):
        return col // 2, 4 * n + (col % 2) * 2 + core

    def quad(d):
        q = (my_q + d) % 4
        return 2 * grp + q % 2, 2 * (col // 2) + q // 2, q

    barrier = pltpu.get_barrier_semaphore()

    def greet(r, c):
        pl.semaphore_signal(barrier, inc=1, device_id=(r, c), device_id_type=MESH)

    greet(row, yp * NZ + z)
    greet(row, ym * NZ + z)

    @pl.when(z < NZ - 1)
    def _():
        greet(row, col + 1)

    @pl.when(z > 0)
    def _():
        greet(row, col - 1)

    for d in range(1, 4):
        qr_, qc_, _q = quad(d)
        greet(qr_, qc_)
    for n in range(8):
        sr_, sc_ = b1_source(n)

        @pl.when(jnp.logical_or(sr_ != row, sc_ != col))
        def _():
            greet(sr_, sc_)

    win = normalize(pair_ref[:QR].astype(F32)).astype(BF16)
    gath[col] = win

    is_own = jnp.logical_and(row == 2 * (row // 2) + col % 2, col == 2 * row + (col // 2) % 2)
    greeted = 2 + 3 + 8 + (z < NZ - 1).astype(jnp.int32) + (z > 0).astype(jnp.int32)
    greeted = greeted - is_own.astype(jnp.int32)
    pl.semaphore_wait(barrier, greeted)

    def hop(direction, s):
        r, c = row, {0: col + 1, 1: col - 1, 2: yp * NZ + z, 3: ym * NZ + z}[direction]
        return pltpu.make_async_remote_copy(
            src_ref=gath.at[s],
            dst_ref=gath.at[s],
            send_sem=send_g.at[direction, s],
            recv_sem=recv_g.at[s],
            device_id=(r, c),
            device_id_type=MESH,
        )

    def arrived(s):
        pltpu.make_async_copy(gath.at[s], gath.at[s], recv_g.at[s]).wait()

    def move(t):
        zr = z - t
        zl = z + t
        sr = y * NZ + zr
        sl = y * NZ + zl

        @pl.when(zr >= 0)
        def _():
            if t > 0:
                arrived(sr)

            @pl.when(z < NZ - 1)
            def _():
                hop(0, sr).start()

            if t == 0:

                @pl.when(z > 0)
                def _():
                    hop(1, sr).start()

            hop(2, sr).start()
            hop(3, sr).start()

        if t > 0:

            @pl.when(zl < NZ)
            def _():
                arrived(sl)

                @pl.when(z > 0)
                def _():
                    hop(1, sl).start()

                hop(2, sl).start()
                hop(3, sl).start()

    def pass_on(t):
        def one(zz):
            @pl.when(zz % 2 == 0)
            def _():
                arrived(ym * NZ + zz)
                hop(2, ym * NZ + zz).start()

            @pl.when(zz % 2 == 1)
            def _():
                arrived(yp * NZ + zz)
                hop(3, yp * NZ + zz).start()

        @pl.when(z - t >= 0)
        def _():
            one(z - t)

        if t > 0:

            @pl.when(z + t < NZ)
            def _():
                one(z + t)

    move(0)

    lane = lax.broadcasted_iota(jnp.int32, (columns, channels), 1)
    head_of = sum((lane >= columns * (h + 1)).astype(jnp.int32) for h in range(HEADS))
    lane_mod = lane - head_of * columns
    lane_w = lax.broadcasted_iota(jnp.int32, (channels, channels), 1)
    wb = wb_ref[...].astype(F32)
    wide = jnp.zeros((channels, channels), F32)
    for h in range(HEADS):
        inside = jnp.logical_and(lane_w >= h * columns, lane_w < (h + 1) * columns)
        wide = jnp.where(inside, wb[:, h : h + 1], wide)
    wide = wide.astype(BF16)
    mask_row = mask_ref[...].astype(F32)
    eye = lax.broadcasted_iota(jnp.int32, (columns, columns), 0) == lax.broadcasted_iota(
        jnp.int32, (columns, columns), 1
    )
    alive = jnp.sum(jnp.where(eye, mask_row, 0.0), axis=1, keepdims=True)
    for half in range(2):
        normed = normalize(pair_ref[half * columns : (half + 1) * columns].astype(F32))
        full = dot(normed.reshape(columns * columns, channels).astype(BF16), wide)
        full = full.reshape(columns, columns, channels)
        picked = jnp.zeros((columns, channels), F32)
        for j in range(columns):
            picked = jnp.where(lane_mod == j, full[j], picked)
        picked = jnp.where(alive > 0.0, picked, DEAD)
        b_own[half] = picked.astype(BF16)

    my_n = col // 4

    def b1_copy(g):
        r, c = b1_dest(g)
        return pltpu.make_async_remote_copy(
            src_ref=b_own,
            dst_ref=part.at[my_n],
            send_sem=send_b1.at[g],
            recv_sem=recv_b1.at[my_n],
            device_id=(r, c),
            device_id_type=MESH,
        )

    def b1_self():
        return pltpu.make_async_copy(b_own, part.at[my_n], recv_b1.at[my_n])

    for g in range(8):
        r_, c_ = b1_dest(g)
        here = jnp.logical_and(r_ == row, c_ == col)

        @pl.when(here)
        def _():
            b1_self().start()

        @pl.when(jnp.logical_not(here))
        def _():
            b1_copy(g).start()

    move(1)
    pass_on(0)

    flat = win.astype(F32).reshape(tokens, channels).astype(BF16)
    q = (dot(flat, wq_ref[...]) * (1.0 / math.sqrt(HEAD_DIM))).astype(BF16)
    lane_t = lax.broadcasted_iota(jnp.int32, (tokens, channels), 1)
    for h in range(HEADS):
        inside = jnp.logical_and(lane_t >= h * HEAD_DIM, lane_t < (h + 1) * HEAD_DIM)
        mine = jnp.where(inside, q.astype(F32), 0.0).astype(BF16)
        qk_h = dot_t(mine, wk_ref[...])
        qk_ref[:, h * columns : (h + 1) * columns, :] = qk_h.reshape(QR, columns, channels)

    for n in range(8):
        pltpu.make_async_copy(part.at[n], part.at[n], recv_b1.at[n]).wait()

    def b2_copy(d):
        r, c, q_ = quad(d)
        return pltpu.make_async_remote_copy(
            src_ref=part.at[:, q_ // 2],
            dst_ref=biasg.at[my_q],
            send_sem=send_b2.at[d],
            recv_sem=recv_b2.at[my_q],
            device_id=(r, c),
            device_id_type=MESH,
        )

    for d in range(1, 4):
        b2_copy(d).start()
    biasg[my_q] = part[:, col % 2]

    for t in range(2, NZ):
        move(t)
        pass_on(t - 1)

    for d in range(1, 4):
        q_ = (my_q + d) % 4
        pltpu.make_async_copy(biasg.at[q_], biasg.at[q_], recv_b2.at[q_]).wait()
    for yy in range(NY):
        block = biasg[:, 2 * yy : 2 * yy + 2].astype(F32)
        block = jnp.swapaxes(block, 0, 1).reshape(NZ * columns, channels)
        bias_t[yy] = jnp.swapaxes(block, 0, 1)[:hq]

    def attend(yy, first):
        def body(step, carry):
            for u in range(4):
                i = step * 4 + u
                block = gath[pl.ds(yy * NZ, NZ), i].astype(F32).reshape(NZ * columns, channels).astype(BF16)
                s = dot_t(qk_ref[i].astype(BF16), block) + bias_t[yy]
                top = jnp.max(s, axis=1, keepdims=True)
                if not first:
                    old = m_ref[i][:, :1]
                    top = jnp.maximum(old, top)
                p = jnp.exp(s - top)
                total = jnp.sum(p, axis=1, keepdims=True)
                weighted = dot(p.astype(BF16), block)
                if not first:
                    factor = jnp.exp(old - top)
                    total = total + l_ref[i][:, :1] * factor
                    weighted = weighted + acc_ref[i] * factor
                m_ref[i] = jnp.broadcast_to(top, (hq, channels))
                l_ref[i] = jnp.broadcast_to(total, (hq, channels))
                acc_ref[i] = weighted
            return carry

        lax.fori_loop(0, QR // 4, body, 0)

    attend(y, True)
    pass_on(NZ - 1)
    for zz in range(1, NZ, 2):
        arrived(ym * NZ + zz)
    attend(ym, False)
    for zz in range(0, NZ, 2):
        arrived(yp * NZ + zz)
    attend(yp, False)
    for zz in range(NZ):
        arrived(y2 * NZ + zz)
    attend(y2, False)

    lane_t = lax.broadcasted_iota(jnp.int32, (tokens, channels), 1)
    mean_n = acc_ref[...] / l_ref[...]
    attended = jnp.zeros((tokens, channels), F32)
    for h in range(HEADS):
        mine = mean_n[:, h * columns : (h + 1) * columns].reshape(tokens, channels).astype(BF16)
        inside = jnp.logical_and(lane_t >= h * HEAD_DIM, lane_t < (h + 1) * HEAD_DIM)
        attended = jnp.where(inside, dot(mine, wv_ref[...]), attended)
    flat = gath[col].astype(F32).reshape(tokens, channels).astype(BF16)
    gated = (sigmoid(dot(flat, wg_ref[...])) * attended).astype(BF16)
    first = pair_ref[:QR].astype(F32).reshape(tokens, channels) + dot(gated, wo_ref[...])
    normed_two = normalize(first).astype(BF16)
    a = dot(normed_two, wha_ref[...])
    b = dot(normed_two, whb_ref[...])
    hidden = (a * sigmoid(a) * b).astype(BF16)
    updated = first + dot(hidden, who_ref[...])
    out_ref[...] = updated.reshape(QR, columns, channels).astype(out_ref.dtype)

    def sent(direction, s):
        pltpu.make_async_copy(gath.at[s], gath.at[s], send_g.at[direction, s]).wait()

    for zz in range(NZ):
        s = y * NZ + zz

        @pl.when(jnp.logical_and(zz <= z, z < NZ - 1))
        def _():
            sent(0, s)

        @pl.when(jnp.logical_and(zz >= z, z > 0))
        def _():
            sent(1, s)

        sent(2, s)
        sent(3, s)
        if zz % 2 == 0:
            sent(2, ym * NZ + zz)
        else:
            sent(3, yp * NZ + zz)
    for g in range(8):
        r_, c_ = b1_dest(g)

        @pl.when(jnp.logical_or(r_ != row, c_ != col))
        def _():
            b1_copy(g).wait_send()

    for d in range(1, 4):
        b2_copy(d).wait_send()


def local(pair, token_mask, *weights):
    rows_block, columns, channels = pair.shape
    hq = HEADS * columns
    cols = NY * NZ
    dma = pltpu.SemaphoreType.DMA
    return pl.pallas_call(
        functools.partial(kernel, columns),
        out_shape=jax.ShapeDtypeStruct((QR, columns, channels), BF16),
        in_specs=[pl.BlockSpec(memory_space=pltpu.VMEM)] * 11,
        out_specs=pl.BlockSpec(memory_space=pltpu.VMEM),
        scratch_shapes=[
            pltpu.VMEM((cols, QR, columns, channels), BF16),
            pltpu.VMEM((8, 2, columns, channels), BF16),
            pltpu.VMEM((4, 8, columns, channels), BF16),
            pltpu.VMEM((NY, hq, NZ * columns), F32),
            pltpu.VMEM((QR, hq, channels), F32),
            pltpu.VMEM((QR, hq, channels), F32),
            pltpu.VMEM((QR, hq, channels), F32),
            pltpu.VMEM((QR, hq, channels), F32),
            pltpu.VMEM((2, columns, channels), BF16),
            dma((4, cols)),
            dma((cols,)),
            dma((8,)),
            dma((8,)),
            dma((4,)),
            dma((4,)),
        ],
        compiler_params=pltpu.CompilerParams(
            collective_id=0, has_side_effects=True, vmem_limit_bytes=48 * 1024 * 1024
        ),
    )(pair, token_mask.reshape(1, columns), *weights)


def solution(mesh):
    return jax.shard_map(
        local,
        mesh=mesh,
        in_specs=(P("row", "col", None), P("col"), P(), P(), P(), P(), P(), P(), P(), P(), P()),
        out_specs=P("row", "col", None),
        check_vma=False,
    )
```

time: 766 us -> 97.5 us (0.13)
  the two profiles are of different devices: /device:TPU:6 before, /device:TPU:10 now
where the time goes in v1:
time: 97.5 us; the launch traced here: 96.9 us
  Pallas kernels  88.2 us (90%)
  local copies, waits for them, and re-layouts  8.69 us (9%)
    pallas_call x1, Pallas kernels, local(): pl.pallas_call(functools.partial(kernel, columns), out_shape=jax.ShapeDty...  88.2 us
    unnamed x24, local copies, waits for them, and re-layouts  8.69 us

profile of v1, /device:TPU:10, one launch (start us, length us, event | category | flops | bytes accessed | tf_op | source)
XLA Modules:
  0.0 96.9 jit_solution(8836184220352260042)
XLA Ops:
  0.0 0.0 copy-start.10
  0.0 0.0 copy-start.4
  0.0 0.7 copy-done.10
  0.7 0.0 copy-start.9
  0.7 0.1 copy.12.wb_ref
  0.8 0.0 copy-done.4
  0.8 0.5 copy-done.9
  1.3 0.0 copy-start
  1.3 1.0 copy-done
  2.3 0.0 copy-start.1
  2.3 0.9 copy-done.1
  3.2 0.0 copy-start.2
  3.2 0.9 copy-done.2
  4.1 0.0 copy-start.3
  4.1 0.9 copy-done.3
  5.0 0.0 copy-start.5
  5.0 0.8 copy-done.5
  5.8 0.0 copy-start.6
  5.8 0.8 copy-done.6
  6.5 0.0 copy-start.7
  6.5 0.8 copy-done.7
  7.3 0.0 copy-start.8
  7.3 0.8 copy-done.8
  8.0 88.2 %shard_map.109 = bf16[20,24,128]{2,1,0:T(8,128)(2,1)S(1)} custom-call(bf16[48,24,128]{2,1,0:T(8,128)(2,1)S(1)} %copy-done, s32[1,24]{1,0:T(1,128)S(1)} %bitcast.1, bf16[128,128]{1,0:T(8,128)(2,1)S(1)} %copy-done.4, bf16[128,128]{1,0:T(8,128)(2,1)S(1)} %copy-done.5, bf16[128,128]{1,0:T(8,128)(2,1)S(1)} %copy-done.6, bf16[128,128]{1,0:T(8,128)(2,1)S(1)} %copy-done.7, ...), custom_call_target="tpu_custom_call" | custom-call | tf_op jit(solution)/shard_map/pallas_call | solution.py:389
  96.3 0.7 copy.14
Async XLA Ops:
  0.0 0.7 copy-start.10
  0.0 0.8 copy-start.4
  0.7 0.7 copy-start.9
  1.3 1.0 copy-start
  2.3 0.9 copy-start.1
  3.2 0.9 copy-start.2
  4.1 0.9 copy-start.3
  5.0 0.8 copy-start.5
  5.8 0.8 copy-start.6
  6.5 0.8 copy-start.7
  7.3 0.8 copy-start.8

commit v2 on v1

--- a/solution.py
+++ b/solution.py
@@ -13,6 +13,8 @@
 QR = 20
 NZ = 8
 NY = 4
+CHUNKS = 1
+UNROLL = 4
 DEAD = -1e30
 MESH = pl.DeviceIdType.MESH
 F32 = jnp.float32
@@ -40,6 +42,34 @@
 
 def kernel(
     columns,
+    *refs,
+):
+    inputs, out_ref, held = refs[:11], refs[11], refs[12:23]
+    pair_ref, mask_ref, wq_ref, wk_ref, wv_ref, wg_ref, wb_ref, wo_ref, wha_ref, whb_ref, who_ref = held
+    body(
+        columns,
+        inputs,
+        held,
+        pair_ref,
+        mask_ref,
+        wq_ref,
+        wk_ref,
+        wv_ref,
+        wg_ref,
+        wb_ref,
+        wo_ref,
+        wha_ref,
+        whb_ref,
+        who_ref,
+        out_ref,
+        *refs[23:],
+    )
+
+
+def body(
+    columns,
+    inputs,
+    held,
     pair_ref,
     mask_ref,
     wq_ref,
@@ -67,6 +97,7 @@
     recv_b1,
     send_b2,
     recv_b2,
+    load_sem,
 ):
     rows_block = pair_ref.shape[0]
     channels = pair_ref.shape[2]
@@ -93,6 +124,17 @@
         q = (my_q + d) % 4
         return 2 * grp + q % 2, 2 * (col // 2) + q // 2, q
 
+    def load(n):
+        if n == 0:
+            return pltpu.make_async_copy(inputs[0].at[:QR], pair_ref.at[:QR], load_sem.at[0])
+        if n == 11:
+            rest = pl.ds(QR, rows_block - QR)
+            return pltpu.make_async_copy(inputs[0].at[rest], pair_ref.at[rest], load_sem.at[11])
+        return pltpu.make_async_copy(inputs[n], held[n], load_sem.at[n])
+
+    for n in (0, 11, 6, 1, 2, 3, 4, 5, 7, 8, 9, 10):
+        load(n).start()
+
     barrier = pltpu.get_barrier_semaphore()
 
     def greet(r, c):
@@ -119,6 +161,7 @@
         def _():
             greet(sr_, sc_)
 
+    load(0).wait()
     win = normalize(pair_ref[:QR].astype(F32)).astype(BF16)
     gath[col] = win
 
@@ -205,13 +248,11 @@
     lane = lax.broadcasted_iota(jnp.int32, (columns, channels), 1)
     head_of = sum((lane >= columns * (h + 1)).astype(jnp.int32) for h in range(HEADS))
     lane_mod = lane - head_of * columns
-    lane_w = lax.broadcasted_iota(jnp.int32, (channels, channels), 1)
+    for n in (11, 6, 1):
+        load(n).wait()
     wb = wb_ref[...].astype(F32)
-    wide = jnp.zeros((channels, channels), F32)
-    for h in range(HEADS):
-        inside = jnp.logical_and(lane_w >= h * columns, lane_w < (h + 1) * columns)
-        wide = jnp.where(inside, wb[:, h : h + 1], wide)
-    wide = wide.astype(BF16)
+    wide = [jnp.broadcast_to(wb[h : h + 1], (columns, channels)) for h in range(HEADS)]
+    wide = jnp.concatenate(wide + [jnp.zeros((channels - hq, channels), F32)], axis=0).astype(BF16)
     mask_row = mask_ref[...].astype(F32)
     eye = lax.broadcasted_iota(jnp.int32, (columns, columns), 0) == lax.broadcasted_iota(
         jnp.int32, (columns, columns), 1
@@ -219,7 +260,7 @@
     alive = jnp.sum(jnp.where(eye, mask_row, 0.0), axis=1, keepdims=True)
     for half in range(2):
         normed = normalize(pair_ref[half * columns : (half + 1) * columns].astype(F32))
-        full = dot(normed.reshape(columns * columns, channels).astype(BF16), wide)
+        full = dot_t(normed.reshape(columns * columns, channels).astype(BF16), wide)
         full = full.reshape(columns, columns, channels)
         picked = jnp.zeros((columns, channels), F32)
         for j in range(columns):
@@ -258,6 +299,8 @@
     move(1)
     pass_on(0)
 
+    for n in (2, 3):
+        load(n).wait()
     flat = win.astype(F32).reshape(tokens, channels).astype(BF16)
     q = (dot(flat, wq_ref[...]) * (1.0 / math.sqrt(HEAD_DIM))).astype(BF16)
     lane_t = lax.broadcasted_iota(jnp.int32, (tokens, channels), 1)
@@ -292,47 +335,52 @@
     for d in range(1, 4):
         q_ = (my_q + d) % 4
         pltpu.make_async_copy(biasg.at[q_], biasg.at[q_], recv_b2.at[q_]).wait()
-    for yy in range(NY):
-        block = biasg[:, 2 * yy : 2 * yy + 2].astype(F32)
-        block = jnp.swapaxes(block, 0, 1).reshape(NZ * columns, channels)
-        bias_t[yy] = jnp.swapaxes(block, 0, 1)[:hq]
-
-    def attend(yy, first):
-        def body(step, carry):
-            for u in range(4):
-                i = step * 4 + u
-                block = gath[pl.ds(yy * NZ, NZ), i].astype(F32).reshape(NZ * columns, channels).astype(BF16)
-                s = dot_t(qk_ref[i].astype(BF16), block) + bias_t[yy]
-                top = jnp.max(s, axis=1, keepdims=True)
-                if not first:
-                    old = m_ref[i][:, :1]
-                    top = jnp.maximum(old, top)
-                p = jnp.exp(s - top)
-                total = jnp.sum(p, axis=1, keepdims=True)
-                weighted = dot(p.astype(BF16), block)
-                if not first:
-                    factor = jnp.exp(old - top)
-                    total = total + l_ref[i][:, :1] * factor
-                    weighted = weighted + acc_ref[i] * factor
-                m_ref[i] = jnp.broadcast_to(top, (hq, channels))
-                l_ref[i] = jnp.broadcast_to(total, (hq, channels))
-                acc_ref[i] = weighted
+    wave = NY // CHUNKS
+    keys = wave * NZ * columns
+    for part_no in range(CHUNKS):
+        block = biasg[:, 2 * wave * part_no : 2 * wave * (part_no + 1)].astype(F32)
+        block = jnp.swapaxes(block, 0, 1).reshape(keys, channels)
+        bias_t[part_no] = jnp.swapaxes(block, 0, 1)[:hq]
+
+    def attend(part_no, first):
+        def one(i):
+            block = gath[pl.ds(part_no * wave * NZ, wave * NZ), i].astype(F32)
+            block = block.reshape(keys, channels).astype(BF16)
+            s = dot_t(qk_ref[i].astype(BF16), block) + bias_t[part_no]
+            top = jnp.broadcast_to(jnp.max(s, axis=1, keepdims=True), (hq, channels))
+            if not first:
+                old = m_ref[i]
+                top = jnp.maximum(old, top)
+            p = jnp.exp(s - jnp.concatenate([top] * (keys // channels), axis=1))
+            total = jnp.broadcast_to(jnp.sum(p, axis=1, keepdims=True), (hq, channels))
+            weighted = dot(p.astype(BF16), block)
+            if not first:
+                factor = jnp.exp(old - top)
+                total = total + l_ref[i] * factor
+                weighted = weighted + acc_ref[i] * factor
+            if CHUNKS > 1 and first:
+                m_ref[i] = top
+            l_ref[i] = total
+            acc_ref[i] = weighted
+
+        def several(step, carry):
+            for u in range(UNROLL):
+                one(step * UNROLL + u)
             return carry
 
-        lax.fori_loop(0, QR // 4, body, 0)
-
-    attend(y, True)
+        lax.fori_loop(0, QR // UNROLL, several, 0)
+
     pass_on(NZ - 1)
     for zz in range(1, NZ, 2):
         arrived(ym * NZ + zz)
-    attend(ym, False)
     for zz in range(0, NZ, 2):
         arrived(yp * NZ + zz)
-    attend(yp, False)
     for zz in range(NZ):
         arrived(y2 * NZ + zz)
-    attend(y2, False)
-
+    attend(0, True)
+
+    for n in (4, 5, 7, 8, 9, 10):
+        load(n).wait()
     lane_t = lax.broadcasted_iota(jnp.int32, (tokens, channels), 1)
     mean_n = acc_ref[...] / l_ref[...]
     attended = jnp.zeros((tokens, channels), F32)
@@ -381,7 +429,8 @@
         b2_copy(d).wait_send()
 
 
-def local(pair, token_mask, *weights):
+def local(pair, token_mask, w_query, w_key, w_value, w_gate, w_bias, *others):
+    inputs = (pair, token_mask.reshape(1, -1), w_query, w_key, w_value, w_gate, w_bias.T, *others)
     rows_block, columns, channels = pair.shape
     hq = HEADS * columns
     cols = NY * NZ
@@ -389,13 +438,14 @@
     return pl.pallas_call(
         functools.partial(kernel, columns),
         out_shape=jax.ShapeDtypeStruct((QR, columns, channels), BF16),
-        in_specs=[pl.BlockSpec(memory_space=pltpu.VMEM)] * 11,
+        in_specs=[pl.BlockSpec(memory_space=pltpu.HBM)] * 11,
         out_specs=pl.BlockSpec(memory_space=pltpu.VMEM),
-        scratch_shapes=[
+        scratch_shapes=[pltpu.VMEM(array.shape, array.dtype) for array in inputs]
+        + [
             pltpu.VMEM((cols, QR, columns, channels), BF16),
             pltpu.VMEM((8, 2, columns, channels), BF16),
             pltpu.VMEM((4, 8, columns, channels), BF16),
-            pltpu.VMEM((NY, hq, NZ * columns), F32),
+            pltpu.VMEM((CHUNKS, hq, cols * columns // CHUNKS), F32),
             pltpu.VMEM((QR, hq, channels), F32),
             pltpu.VMEM((QR, hq, channels), F32),
             pltpu.VMEM((QR, hq, channels), F32),
@@ -407,11 +457,12 @@
             dma((8,)),
             dma((4,)),
             dma((4,)),
+            dma((12,)),
         ],
         compiler_params=pltpu.CompilerParams(
-            collective_id=0, has_side_effects=True, vmem_limit_bytes=48 * 1024 * 1024
+            collective_id=0, has_side_effects=True, vmem_limit_bytes=64 * 1024 * 1024
         ),
-    )(pair, token_mask.reshape(1, columns), *weights)
+    )(*inputs)
 
 
 def solution(mesh):

time: 97.5 us -> 74.9 us (0.77)
  the two profiles are of different devices: /device:TPU:10 before, /device:TPU:2 now
where the time goes in v2:
time: 74.9 us; the launch traced here: 74.5 us
  Pallas kernels  73 us (97%)
  local copies, waits for them, and re-layouts  1.56 us (2%)
    pallas_call x1, Pallas kernels, local(): pl.pallas_call(functools.partial(kernel, columns), out_shape=jax.ShapeDty...  73 us
    unnamed x1, local copies, waits for them, and re-layouts  1.56 us

profile of v2, /device:TPU:2, one launch (start us, length us, event | category | flops | bytes accessed | tf_op | source)
XLA Modules:
  0.0 74.5 jit_solution(13231131524843667099)
XLA Ops:
  0.0 73.0 %shard_map.109 = bf16[20,24,128]{2,1,0:T(8,128)(2,1)} custom-call(bf16[48,24,128]{2,1,0:T(8,128)(2,1)} %refs_0_.1, s32[1,24]{1,0:T(1,128)} %bitcast.3, bf16[128,128]{1,0:T(8,128)(2,1)} %refs_2_.1, bf16[128,128]{1,0:T(8,128)(2,1)} %refs_3_.1, bf16[128,128]{1,0:T(8,128)(2,1)} %refs_4_.1, bf16[128,128]{1,0:T(8,128)(2,1)} %refs_5_.1, bf16[4,128]{1,0:T(4,128)(2,1)} %bitcast.2, ...), custom_call_target="tpu_custom_call" | custom-call | tf_op jit(solution)/shard_map/pallas_call | solution.py:438
  73.0 1.6 %copy.13 = bf16[20,24,128]{2,1,0:T(8,128)(2,1)} copy(bf16[20,24,128]{2,1,0:T(8,128)(2,1)} %shard_map.109) | data formatting | bytes 245760

commit v3 on v0

v3 whole, which is shorter than its diff:
```python
import functools
import math

import jax
import jax.numpy as jnp
from jax import lax
from jax.experimental import pallas as pl
from jax.experimental.pallas import tpu as pltpu
from jax.sharding import PartitionSpec as P

HEADS = 4
HEAD_DIM = 32
QR = 20
NX = 4
NY = 4
NZ = 8
LINE = 2 * NZ
GROUP = QR // NY
JOINT = 1
DEAD = -1e30
MESH = pl.DeviceIdType.MESH
F32 = jnp.float32
BF16 = jnp.bfloat16


def normalize(values_in):
    average = jnp.mean(values_in, axis=-1, keepdims=True)
    centred = values_in - average
    variance = jnp.mean(centred * centred, axis=-1, keepdims=True)
    return centred * lax.rsqrt(variance + 1e-05)


def dot(a, b):
    return jnp.dot(a, b, preferred_element_type=F32)


def dot_t(a, b):
    return lax.dot_general(a, b, (((1,), (1,)), ((), ())), preferred_element_type=F32)


def sigmoid(v):
    return 1.0 / (1.0 + jnp.exp(-v))


def kernel(columns, *refs):
    inputs, out_ref, held = refs[:11], refs[11], refs[12:23]
    pair_ref, mask_ref, wq_ref, wk_ref, wv_ref, wg_ref, wb_ref, wo_ref, wha_ref, whb_ref, who_ref = held
    gath, own, gated_ref, back, turned, bias_all, bias_t, qk_ref, mean_ref = refs[23:32]
    send_o, send_g, recv_g, recv_p, send_r, recv_r, turn_sem, send_z, recv_z = refs[32:41]
    send_b, recv_b, core_sem, walk_sem, load_sem = refs[41:]
    rows_block, _, channels = pair_ref.shape
    tokens = QR * columns
    hq = HEADS * columns
    keys = NY * NZ * columns
    row = lax.axis_index("row")
    col = lax.axis_index("col")
    x, zh, core = row // 4, (row // 2) % 2, row % 2
    y, z = col // NZ, col % NZ
    place = zh * NZ + z

    def at_x(other):
        return other * 4 + zh * 2 + core, col

    def at_y(other):
        return row, other * NZ + z

    def at_place(other):
        return x * 4 + (other // NZ) * 2 + core, y * NZ + other % NZ

    sibling = (row + 1 - 2 * core, col)
    mirror = (y * 4 + zh * 2 + core, x * NZ + z)

    def load(n):
        if n == 0:
            return pltpu.make_async_copy(inputs[0].at[:QR], pair_ref.at[:QR], load_sem.at[0])
        if n == 11:
            rest_rows = pl.ds(QR, rows_block - QR)
            return pltpu.make_async_copy(inputs[0].at[rest_rows], pair_ref.at[rest_rows], load_sem.at[11])
        return pltpu.make_async_copy(inputs[n], held[n], load_sem.at[n])

    barrier = pltpu.get_barrier_semaphore()

    def tell(sem, target):
        pl.semaphore_signal(sem, inc=1, device_id=target, device_id_type=MESH)

    def either_side(distance, fn):
        @pl.when(place >= distance)
        def _():
            fn(0, place - distance)

        @pl.when(place + distance < LINE)
        def _():
            fn(1, place + distance)

    for d in range(1, NY):
        tell(barrier, at_y((y + d) % NY))
    for d in range(1, NX):
        tell(barrier, at_x((x + d) % NX))
    tell(barrier, sibling)

    @pl.when(x != y)
    def _():
        tell(barrier, mirror)

    either_side(1, lambda side, other: tell(barrier, at_place(other)))
    for n in (0, 11, 6, 1, 2, 3, 4, 5, 7, 8, 9, 10):
        load(n).start()
    load(0).wait()
    win = normalize(pair_ref[:QR].astype(F32)).astype(BF16)
    own[...] = win.reshape(NY, GROUP, columns, channels)
    gath[y, z] = own[y]
    greeted = (place > 0).astype(jnp.int32) + (place < LINE - 1).astype(jnp.int32) + (x != y).astype(jnp.int32)
    pl.semaphore_wait(barrier, NX + NY - 1 + greeted)

    def walk_tell(n):
        either_side(2**n, lambda side, other: tell(walk_sem.at[n, 1 - side], at_place(other)))

    def walk_wait(n):
        either_side(2**n, lambda side, other: pl.semaphore_wait(walk_sem.at[n, side], 1))

    def local_wait(ref, sem):
        pltpu.make_async_copy(ref, ref, sem).wait()

    def remote(src, dst, send, recv, target):
        return pltpu.make_async_remote_copy(
            src_ref=src, dst_ref=dst, send_sem=send, recv_sem=recv, device_id=target, device_id_type=MESH
        )

    def spread(other):
        return remote(own.at[other], gath.at[y, z], send_o.at[other], recv_g.at[y], at_y(other))

    def piece(p, zz):
        return gath.at[pl.ds(p * JOINT, JOINT), zz]

    def hop(side, p, zz):
        target = (row, col - 1 + 2 * side)
        return remote(piece(p, zz), piece(p, zz), send_g.at[side, p, zz], recv_p.at[p, zz], target)

    def begin(p):
        @pl.when(z < NZ - 1)
        def _():
            hop(1, p, z).start()

        @pl.when(z > 0)
        def _():
            hop(0, p, z).start()

    def step(t):
        def one(o, carry):
            p = (y // JOINT + o) % (NY // JOINT)

            @pl.when(z >= t)
            def _():
                local_wait(piece(p, z - t), recv_p.at[p, z - t])

                @pl.when(z < NZ - 1)
                def _():
                    hop(1, p, z - t).start()

            @pl.when(z + t < NZ)
            def _():
                local_wait(piece(p, z + t), recv_p.at[p, z + t])

                @pl.when(z > 0)
                def _():
                    hop(0, p, z + t).start()

            return carry

        lax.fori_loop(0, NY // JOINT, one, 0)

    walk_tell(0)
    begin(y)
    for d in (1, 3, 2):
        spread((y + d) % NY).start()

    lane = lax.broadcasted_iota(jnp.int32, (columns, channels), 1)
    head_of = sum((lane >= columns * (h + 1)).astype(jnp.int32) for h in range(HEADS))
    lane_mod = lane - head_of * columns
    for n in (11, 6, 1):
        load(n).wait()
    wb = wb_ref[...].astype(F32)
    wide = [jnp.broadcast_to(wb[h : h + 1], (columns, channels)) for h in range(HEADS)]
    wide = jnp.concatenate(wide + [jnp.zeros((channels - hq, channels), F32)], axis=0).astype(BF16)
    mask_row = mask_ref[...].astype(F32)
    eye = lax.broadcasted_iota(jnp.int32, (columns, columns), 0) == lax.broadcasted_iota(
        jnp.int32, (columns, columns), 1
    )
    alive = jnp.sum(jnp.where(eye, mask_row, 0.0), axis=1, keepdims=True)
    for half in range(2):
        normed = normalize(pair_ref[half * columns : (half + 1) * columns].astype(F32))
        full = dot_t(normed.reshape(columns * columns, channels).astype(BF16), wide)
        full = full.reshape(columns, columns, channels)
        picked = jnp.zeros((columns, channels), F32)
        for j in range(columns):
            picked = jnp.where(lane_mod == j, full[j], picked)
        picked = jnp.where(alive > 0.0, picked, DEAD)
        turned[0, half] = picked.astype(BF16)

    def turn():
        return remote(turned.at[0], turned.at[1], turn_sem.at[0], turn_sem.at[1], mirror)

    def z_place(half, far):
        return far * NZ + zh * 4 + core * 2 + half

    def copy_z(half, far):
        target = at_place(z_place(half, far))
        return remote(turned.at[1, half], bias_all.at[y, x, z], send_z.at[half, far], recv_z.at[z], target)

    low, high = pl.ds(0, NZ // 2), pl.ds(NZ // 2, NZ // 2)

    def plane(n, other):
        part = (
            bias_all.at[y, x, low],
            bias_all.at[y, x, high],
            bias_all.at[y, :, low],
            bias_all.at[:, x, high],
        )[n]
        mine = y if n in (1, 2) else x
        target = at_y(other) if n in (1, 2) else at_x(other)
        return remote(part, part, send_b.at[n, other], recv_b.at[n, mine], target)

    def plane_wait(n, other):
        part = (
            bias_all.at[y, other, low],
            bias_all.at[other, x, high],
            bias_all.at[other, :, low],
            bias_all.at[:, other, high],
        )[n]
        local_wait(part, recv_b.at[n, other])

    def others(n):
        return [((y if n in (1, 2) else x) + d) % NY for d in (1, 3, 2)]

    def copy_c():
        return remote(bias_all, bias_all, core_sem.at[0], core_sem.at[1], sibling)

    @pl.when(x != y)
    def _():
        turn().start()

    @pl.when(x == y)
    def _():
        pltpu.make_async_copy(turned.at[0], turned.at[1], turn_sem.at[1]).start()

    walk_wait(0)
    walk_tell(1)
    for d in (1, 3, 2):
        p = (y + d) % NY
        local_wait(gath.at[p, z], recv_g.at[p])
        begin(p)
    walk_wait(1)
    walk_tell(2)
    step(1)
    local_wait(turned.at[1], turn_sem.at[1])
    walk_wait(2)
    walk_tell(3)

    for n in (2, 3):
        load(n).wait()
    flat = gath[:, z].astype(F32).reshape(tokens, channels).astype(BF16)
    q = (dot(flat, wq_ref[...]) * (1.0 / math.sqrt(HEAD_DIM))).astype(BF16)
    lane_t = lax.broadcasted_iota(jnp.int32, (tokens, channels), 1)
    for h in range(HEADS):
        inside = jnp.logical_and(lane_t >= h * HEAD_DIM, lane_t < (h + 1) * HEAD_DIM)
        mine = jnp.where(inside, q.astype(F32), 0.0).astype(BF16)
        qk_h = dot_t(mine, wk_ref[...])
        qk_ref[:, :, h * columns : (h + 1) * columns, :] = qk_h.reshape(NY, GROUP, columns, channels)

    step(2)
    walk_wait(3)
    for half in range(2):
        for far in range(2):
            here = z_place(half, far) == place

            @pl.when(here)
            def _():
                pltpu.make_async_copy(turned.at[1, half], bias_all.at[y, x, z], recv_z.at[z]).start()

            @pl.when(jnp.logical_not(here))
            def _():
                copy_z(half, far).start()

    owner = core == (z // 2) % 2
    step(3)
    step(4)

    @pl.when(owner)
    def _():
        for zz in range(NZ):
            local_wait(bias_all.at[y, x, zz], recv_z.at[zz])
        for n in (0, 1):
            for other in others(n):
                plane(n, other).start()

    step(5)

    @pl.when(owner)
    def _():
        for n in (0, 1):
            for other in others(n):
                plane_wait(n, other)
        for n in (2, 3):
            for other in others(n):
                plane(n, other).start()

    step(6)

    @pl.when(owner)
    def _():
        for n in (2, 3):
            for other in others(n):
                plane_wait(n, other)
        copy_c().start()

    step(7)

    @pl.when(jnp.logical_not(owner))
    def _():
        local_wait(bias_all, core_sem.at[1])

    for n in range(NY):
        block = bias_all[n].astype(F32).reshape(keys, channels)
        bias_t[n] = jnp.swapaxes(block, 0, 1)[:hq]

    def attend(i, carry):
        block = gath[:, :, i].astype(F32).reshape(keys, channels).astype(BF16)
        for n in range(NY):
            s = dot_t(qk_ref[n, i].astype(BF16), block) + bias_t[n]
            prob = jnp.exp(s - jnp.max(s, axis=1, keepdims=True))
            total = jnp.sum(prob, axis=1, keepdims=True)
            mean_ref[n, i] = dot(prob.astype(BF16), block) / total
        return carry

    lax.fori_loop(0, GROUP, attend, 0)

    for n in (4, 5, 7, 8, 9, 10):
        load(n).wait()
    attended = jnp.zeros((tokens, channels), F32)
    for h in range(HEADS):
        mine = mean_ref[:, :, h * columns : (h + 1) * columns].reshape(tokens, channels).astype(BF16)
        inside = jnp.logical_and(lane_t >= h * HEAD_DIM, lane_t < (h + 1) * HEAD_DIM)
        attended = jnp.where(inside, dot(mine, wv_ref[...]), attended)
    flat = gath[:, z].astype(F32).reshape(tokens, channels).astype(BF16)
    gated = sigmoid(dot(flat, wg_ref[...])) * attended
    gated_ref[...] = gated.reshape(NY, GROUP, columns, channels).astype(BF16)

    def go_home(other):
        return remote(gated_ref.at[other], back.at[y], send_r.at[other], recv_r.at[y], at_y(other))

    for d in (1, 3, 2):
        go_home((y + d) % NY).start()
    back[y] = gated_ref[y]
    for d in (1, 3, 2):
        other = (y + d) % NY
        local_wait(back.at[other], recv_r.at[other])
    gated = back[...].astype(F32).reshape(tokens, channels).astype(BF16)
    first = pair_ref[:QR].astype(F32).reshape(tokens, channels) + dot(gated, wo_ref[...])
    normed_two = normalize(first).astype(BF16)
    a = dot(normed_two, wha_ref[...])
    b = dot(normed_two, whb_ref[...])
    hidden = (a * sigmoid(a) * b).astype(BF16)
    updated = first + dot(hidden, who_ref[...])
    out_ref[...] = updated.reshape(QR, columns, channels).astype(out_ref.dtype)

    for d in range(1, NY):
        spread((y + d) % NY).wait_send()
        go_home((y + d) % NY).wait_send()

    def left(p, carry):
        for zz in range(NZ):

            @pl.when(jnp.logical_and(zz <= z, z < NZ - 1))
            def _():
                local_wait(piece(p, zz), send_g.at[1, p, zz])

            @pl.when(jnp.logical_and(zz >= z, z > 0))
            def _():
                local_wait(piece(p, zz), send_g.at[0, p, zz])

        return carry

    lax.fori_loop(0, NY // JOINT, left, 0)

    @pl.when(x != y)
    def _():
        turn().wait_send()

    for half in range(2):
        for far in range(2):

            @pl.when(z_place(half, far) != place)
            def _():
                copy_z(half, far).wait_send()

    @pl.when(owner)
    def _():
        for n in range(4):
            for other in others(n):
                plane(n, other).wait_send()
        copy_c().wait_send()


def local(pair, token_mask, w_query, w_key, w_value, w_gate, w_bias, *others):
    inputs = (pair, token_mask.reshape(1, -1), w_query, w_key, w_value, w_gate, w_bias.T, *others)
    rows_block, columns, channels = pair.shape
    hq = HEADS * columns
    cols = NY * NZ
    dma = pltpu.SemaphoreType.DMA
    return pl.pallas_call(
        functools.partial(kernel, columns),
        out_shape=jax.ShapeDtypeStruct((QR, columns, channels), BF16),
        in_specs=[pl.BlockSpec(memory_space=pltpu.HBM)] * 11,
        out_specs=pl.BlockSpec(memory_space=pltpu.VMEM),
        scratch_shapes=[pltpu.VMEM(array.shape, array.dtype) for array in inputs]
        + [
            pltpu.VMEM((NY, NZ, GROUP, columns, channels), BF16),
            pltpu.VMEM((NY, GROUP, columns, channels), BF16),
            pltpu.VMEM((NY, GROUP, columns, channels), BF16),
            pltpu.VMEM((NY, GROUP, columns, channels), BF16),
            pltpu.VMEM((2, 2, columns, channels), BF16),
            pltpu.VMEM((NY, NX, NZ, columns, channels), BF16),
            pltpu.VMEM((NY, hq, cols * columns), F32),
            pltpu.VMEM((NY, GROUP, hq, channels), F32),
            pltpu.VMEM((NY, GROUP, hq, channels), F32),
            dma((NY,)),
            dma((2, NY // JOINT, NZ)),
            dma((NY,)),
            dma((NY // JOINT, NZ)),
            dma((NY,)),
            dma((NY,)),
            dma((2,)),
            dma((2, 2)),
            dma((NZ,)),
            dma((4, NY)),
            dma((4, NY)),
            dma((2,)),
            pltpu.SemaphoreType.REGULAR((4, 2)),
            dma((12,)),
        ],
        compiler_params=pltpu.CompilerParams(
            collective_id=0, has_side_effects=True, vmem_limit_bytes=48 * 1024 * 1024
        ),
    )(*[pltpu.with_memory_space_constraint(array, pltpu.HBM) for array in inputs])


def solution(mesh):
    return jax.shard_map(
        local,
        mesh=mesh,
        in_specs=(P("row", "col", None), P("col"), P(), P(), P(), P(), P(), P(), P(), P(), P()),
        out_specs=P("row", "col", None),
        check_vma=False,
    )
```

time: 766 us -> 59.4 us (0.08)
  the two profiles are of different devices: /device:TPU:6 before, /device:TPU:1 now
where the time goes in v3:
time: 59.4 us; the launch traced here: 59.3 us
  Pallas kernels  58.6 us (99%)
  local copies, waits for them, and re-layouts  0.65 us (1%)
    pallas_call x1, Pallas kernels, local(): pl.pallas_call(functools.partial(kernel, columns), out_shape=jax.ShapeDty...  58.6 us

profile of v3, /device:TPU:1, one launch (start us, length us, event | category | flops | bytes accessed | tf_op | source)
XLA Modules:
  0.0 59.3 jit_solution(15497823459932597590)
XLA Ops:
  0.0 58.6 %shard_map.109 = bf16[20,24,128]{2,1,0:T(8,128)(2,1)S(1)} custom-call(bf16[48,24,128]{2,1,0:T(8,128)(2,1)} %refs_0_.1, s32[1,24]{1,0:T(1,128)} %bitcast.3, bf16[128,128]{1,0:T(8,128)(2,1)} %refs_2_.1, bf16[128,128]{1,0:T(8,128)(2,1)} %refs_3_.1, bf16[128,128]{1,0:T(8,128)(2,1)} %refs_4_.1, bf16[128,128]{1,0:T(8,128)(2,1)} %refs_5_.1, ...), custom_call_target="tpu_custom_call" | custom-call | tf_op jit(solution)/shard_map/pallas_call | solution.py:410
  58.6 0.7 %copy.13 = bf16[20,24,128]{2,1,0:T(8,128)(2,1)} copy(bf16[20,24,128]{2,1,0:T(8,128)(2,1)S(1)} %shard_map.109) | data formatting | bytes 245760

commit v4 on v3

--- a/solution.py
+++ b/solution.py
@@ -47,7 +47,7 @@
     pair_ref, mask_ref, wq_ref, wk_ref, wv_ref, wg_ref, wb_ref, wo_ref, wha_ref, whb_ref, who_ref = held
     gath, own, gated_ref, back, turned, bias_all, bias_t, qk_ref, mean_ref = refs[23:32]
     send_o, send_g, recv_g, recv_p, send_r, recv_r, turn_sem, send_z, recv_z = refs[32:41]
-    send_b, recv_b, core_sem, walk_sem, load_sem = refs[41:]
+    send_b, recv_b, send_c, recv_c, walk_sem, load_sem = refs[41:]
     rows_block, _, channels = pair_ref.shape
     tokens = QR * columns
     hq = HEADS * columns
@@ -232,8 +232,22 @@
     def others(n):
         return [((y if n in (1, 2) else x) + d) % NY for d in (1, 3, 2)]
 
-    def copy_c():
-        return remote(bias_all, bias_all, core_sem.at[0], core_sem.at[1], sibling)
+    def across(n, other):
+        return bias_all.at[:, other, high] if n else bias_all.at[other, :, low]
+
+    def copy_c(n, other):
+        return remote(across(n, other), across(n, other), send_c.at[n, other], recv_c.at[n, other], sibling)
+
+    def line_send(half, far):
+        here = z_place(half, far) == place
+
+        @pl.when(here)
+        def _():
+            pltpu.make_async_copy(turned.at[1, half], bias_all.at[y, x, z], recv_z.at[z]).start()
+
+        @pl.when(jnp.logical_not(here))
+        def _():
+            copy_z(half, far).start()
 
     @pl.when(x != y)
     def _():
@@ -251,10 +265,12 @@
         begin(p)
     walk_wait(1)
     walk_tell(2)
-    step(1)
     local_wait(turned.at[1], turn_sem.at[1])
     walk_wait(2)
     walk_tell(3)
+    for half in range(2):
+        line_send(half, zh)
+    step(1)
 
     for n in (2, 3):
         load(n).wait()
@@ -270,69 +286,72 @@
     step(2)
     walk_wait(3)
     for half in range(2):
-        for far in range(2):
-            here = z_place(half, far) == place
-
-            @pl.when(here)
-            def _():
-                pltpu.make_async_copy(turned.at[1, half], bias_all.at[y, x, z], recv_z.at[z]).start()
-
-            @pl.when(jnp.logical_not(here))
-            def _():
-                copy_z(half, far).start()
-
+        line_send(half, 1 - zh)
     owner = core == (z // 2) % 2
-    step(3)
-    step(4)
-
-    @pl.when(owner)
-    def _():
+    soon = z // 4 == zh
+
+    def plane_one():
         for zz in range(NZ):
             local_wait(bias_all.at[y, x, zz], recv_z.at[zz])
         for n in (0, 1):
             for other in others(n):
                 plane(n, other).start()
 
-    step(5)
-
-    @pl.when(owner)
-    def _():
+    def plane_two():
         for n in (0, 1):
             for other in others(n):
                 plane_wait(n, other)
         for n in (2, 3):
             for other in others(n):
                 plane(n, other).start()
-
+        copy_c(0, y).start()
+        copy_c(1, x).start()
+
+    def to_core():
+        for d in range(NY - 1):
+            for n in (2, 3):
+                other = others(n)[d]
+                plane_wait(n, other)
+                copy_c(n - 2, other).start()
+
+    def stage(t, fn):
+        @pl.when(jnp.logical_and(owner, soon if t else jnp.logical_not(soon)))
+        def _():
+            fn()
+
+    step(3)
+    stage(1, plane_one)
+    step(4)
+    stage(0, plane_one)
+    stage(1, plane_two)
+    step(5)
+    stage(0, plane_two)
+    stage(1, to_core)
     step(6)
-
-    @pl.when(owner)
-    def _():
-        for n in (2, 3):
-            for other in others(n):
-                plane_wait(n, other)
-        copy_c().start()
-
+    stage(0, to_core)
     step(7)
 
     @pl.when(jnp.logical_not(owner))
     def _():
-        local_wait(bias_all, core_sem.at[1])
+        for n in range(2):
+            for other in range(NY):
+                local_wait(across(n, other), recv_c.at[n, other])
 
     for n in range(NY):
         block = bias_all[n].astype(F32).reshape(keys, channels)
         bias_t[n] = jnp.swapaxes(block, 0, 1)[:hq]
 
-    def attend(i, carry):
+    def attend(i):
         block = gath[:, :, i].astype(F32).reshape(keys, channels).astype(BF16)
-        for n in range(NY):
-            s = dot_t(qk_ref[n, i].astype(BF16), block) + bias_t[n]
-            prob = jnp.exp(s - jnp.max(s, axis=1, keepdims=True))
-            total = jnp.sum(prob, axis=1, keepdims=True)
-            mean_ref[n, i] = dot(prob.astype(BF16), block) / total
-        return carry
-
-    lax.fori_loop(0, GROUP, attend, 0)
+        qk = qk_ref[:, i].reshape(NY * hq, channels).astype(BF16)
+        s = dot_t(qk, block) + bias_t[...].reshape(NY * hq, keys)
+        prob = jnp.exp(s - jnp.max(s, axis=1, keepdims=True))
+        total = jnp.sum(prob, axis=1, keepdims=True)
+        mean = dot(prob.astype(BF16), block) / total
+        mean_ref[:, i] = mean.reshape(NY, hq, channels)
+
+    for i in range(GROUP):
+        attend(i)
 
     for n in (4, 5, 7, 8, 9, 10):
         load(n).wait()
@@ -398,7 +417,9 @@
         for n in range(4):
             for other in others(n):
                 plane(n, other).wait_send()
-        copy_c().wait_send()
+        for n in range(2):
+            for other in range(NY):
+                copy_c(n, other).wait_send()
 
 
 def local(pair, token_mask, w_query, w_key, w_value, w_gate, w_bias, *others):
@@ -434,7 +455,8 @@
             dma((NZ,)),
             dma((4, NY)),
             dma((4, NY)),
-            dma((2,)),
+            dma((2, NY)),
+            dma((2, NY)),
             pltpu.SemaphoreType.REGULAR((4, 2)),
             dma((12,)),
         ],

time: 59.4 us -> 53 us (0.89)
  the two profiles are of different devices: /device:TPU:1 before, /device:TPU:2 now
where the time goes in v4:
time: 53 us; the launch traced here: 52.9 us
  Pallas kernels  52.2 us (98%)
  local copies, waits for them, and re-layouts  0.65 us (1%)
    pallas_call x1, Pallas kernels, local(): pl.pallas_call(functools.partial(kernel, columns), out_shape=jax.ShapeDty...  52.2 us

profile of v4, /device:TPU:2, one launch (start us, length us, event | category | flops | bytes accessed | tf_op | source)
XLA Modules:
  0.0 52.9 jit_solution(3530690550789771395)
XLA Ops:
  0.0 52.2 %shard_map.109 = bf16[20,24,128]{2,1,0:T(8,128)(2,1)S(1)} custom-call(bf16[48,24,128]{2,1,0:T(8,128)(2,1)} %refs_0_.1, s32[1,24]{1,0:T(1,128)} %bitcast.3, bf16[128,128]{1,0:T(8,128)(2,1)} %refs_2_.1, bf16[128,128]{1,0:T(8,128)(2,1)} %refs_3_.1, bf16[128,128]{1,0:T(8,128)(2,1)} %refs_4_.1, bf16[128,128]{1,0:T(8,128)(2,1)} %refs_5_.1, ...), custom_call_target="tpu_custom_call" | custom-call | tf_op jit(solution)/shard_map/pallas_call | solution.py:431
  52.2 0.7 %copy.13 = bf16[20,24,128]{2,1,0:T(8,128)(2,1)} copy(bf16[20,24,128]{2,1,0:T(8,128)(2,1)S(1)} %shard_map.109) | data formatting | bytes 245760

commit v5 on v4

--- a/solution.py
+++ b/solution.py
@@ -14,7 +14,6 @@
 NX = 4
 NY = 4
 NZ = 8
-LINE = 2 * NZ
 GROUP = QR // NY
 JOINT = 1
 DEAD = -1e30
@@ -47,7 +46,7 @@
     pair_ref, mask_ref, wq_ref, wk_ref, wv_ref, wg_ref, wb_ref, wo_ref, wha_ref, whb_ref, who_ref = held
     gath, own, gated_ref, back, turned, bias_all, bias_t, qk_ref, mean_ref = refs[23:32]
     send_o, send_g, recv_g, recv_p, send_r, recv_r, turn_sem, send_z, recv_z = refs[32:41]
-    send_b, recv_b, send_c, recv_c, walk_sem, load_sem = refs[41:]
+    send_b, recv_b, send_c, recv_c, far_sem, ready_sem, load_sem = refs[41:]
     rows_block, _, channels = pair_ref.shape
     tokens = QR * columns
     hq = HEADS * columns
@@ -83,14 +82,26 @@
     def tell(sem, target):
         pl.semaphore_signal(sem, inc=1, device_id=target, device_id_type=MESH)
 
-    def either_side(distance, fn):
-        @pl.when(place >= distance)
-        def _():
-            fn(0, place - distance)
-
-        @pl.when(place + distance < LINE)
-        def _():
-            fn(1, place + distance)
+    def z_place(half, far):
+        return far * NZ + zh * 4 + core * 2 + half
+
+    owner = core == (z // 2) % 2
+    near = z // 4 == zh
+    giver = jnp.logical_and(owner, jnp.logical_and(z < NZ // 2, zh == 0))
+    getter = jnp.logical_and(owner, jnp.logical_and(z < NZ // 2, zh == 1))
+
+    @pl.when(jnp.logical_and(owner, near))
+    def _():
+        for zz in range(NZ):
+
+            @pl.when(zz != z)
+            def _():
+                tell(barrier, at_place(zh * NZ + zz))
+
+    @pl.when(jnp.logical_and(owner, jnp.logical_and(z >= NZ // 2, zh == 0)))
+    def _():
+        for zz in range(NZ):
+            tell(barrier, at_place(NZ + zz))
 
     for d in range(1, NY):
         tell(barrier, at_y((y + d) % NY))
@@ -102,21 +113,29 @@
     def _():
         tell(barrier, mirror)
 
-    either_side(1, lambda side, other: tell(barrier, at_place(other)))
+
+    @pl.when(z > 0)
+    def _():
+        tell(barrier, (row, col - 1))
+
+    @pl.when(z < NZ - 1)
+    def _():
+        tell(barrier, (row, col + 1))
+
+    @pl.when(giver)
+    def _():
+        tell(barrier, at_place(NZ + z))
+
     for n in (0, 11, 6, 1, 2, 3, 4, 5, 7, 8, 9, 10):
         load(n).start()
     load(0).wait()
     win = normalize(pair_ref[:QR].astype(F32)).astype(BF16)
     own[...] = win.reshape(NY, GROUP, columns, channels)
     gath[y, z] = own[y]
-    greeted = (place > 0).astype(jnp.int32) + (place < LINE - 1).astype(jnp.int32) + (x != y).astype(jnp.int32)
+    greeted = (z > 0).astype(jnp.int32) + (z < NZ - 1).astype(jnp.int32) + (x != y).astype(jnp.int32)
+    greeted = greeted + getter.astype(jnp.int32)
+    greeted = greeted + 2 + 2 * zh - jnp.logical_and(owner, near).astype(jnp.int32)
     pl.semaphore_wait(barrier, NX + NY - 1 + greeted)
-
-    def walk_tell(n):
-        either_side(2**n, lambda side, other: tell(walk_sem.at[n, 1 - side], at_place(other)))
-
-    def walk_wait(n):
-        either_side(2**n, lambda side, other: pl.semaphore_wait(walk_sem.at[n, side], 1))
 
     def local_wait(ref, sem):
         pltpu.make_async_copy(ref, ref, sem).wait()
@@ -169,10 +188,13 @@
 
         lax.fori_loop(0, NY // JOINT, one, 0)
 
-    walk_tell(0)
-    begin(y)
+    @pl.when(getter)
+    def _():
+        tell(ready_sem, at_place(z))
+
     for d in (1, 3, 2):
         spread((y + d) % NY).start()
+    begin(y)
 
     lane = lax.broadcasted_iota(jnp.int32, (columns, channels), 1)
     head_of = sum((lane >= columns * (h + 1)).astype(jnp.int32) for h in range(HEADS))
@@ -200,9 +222,6 @@
     def turn():
         return remote(turned.at[0], turned.at[1], turn_sem.at[0], turn_sem.at[1], mirror)
 
-    def z_place(half, far):
-        return far * NZ + zh * 4 + core * 2 + half
-
     def copy_z(half, far):
         target = at_place(z_place(half, far))
         return remote(turned.at[1, half], bias_all.at[y, x, z], send_z.at[half, far], recv_z.at[z], target)
@@ -257,19 +276,19 @@
     def _():
         pltpu.make_async_copy(turned.at[0], turned.at[1], turn_sem.at[1]).start()
 
-    walk_wait(0)
-    walk_tell(1)
     for d in (1, 3, 2):
         p = (y + d) % NY
         local_wait(gath.at[p, z], recv_g.at[p])
         begin(p)
-    walk_wait(1)
-    walk_tell(2)
     local_wait(turned.at[1], turn_sem.at[1])
-    walk_wait(2)
-    walk_tell(3)
     for half in range(2):
         line_send(half, zh)
+
+    @pl.when(zh == 1)
+    def _():
+        for half in range(2):
+            line_send(half, 0)
+
     step(1)
 
     for n in (2, 3):
@@ -283,16 +302,24 @@
         qk_h = dot_t(mine, wk_ref[...])
         qk_ref[:, :, h * columns : (h + 1) * columns, :] = qk_h.reshape(NY, GROUP, columns, channels)
 
-    step(2)
-    walk_wait(3)
-    for half in range(2):
-        line_send(half, 1 - zh)
-    owner = core == (z // 2) % 2
-    soon = z // 4 == zh
+    def copy_far():
+        return remote(bias_all.at[y, x], bias_all.at[y, x], far_sem.at[0], far_sem.at[1], at_place(NZ + z))
 
     def plane_one():
-        for zz in range(NZ):
-            local_wait(bias_all.at[y, x, zz], recv_z.at[zz])
+        @pl.when(jnp.logical_not(getter))
+        def _():
+            for zz in range(NZ):
+                local_wait(bias_all.at[y, x, zz], recv_z.at[zz])
+
+        @pl.when(giver)
+        def _():
+            pl.semaphore_wait(ready_sem, 1)
+            copy_far().start()
+
+        @pl.when(getter)
+        def _():
+            local_wait(bias_all.at[y, x], far_sem.at[1])
+
         for n in (0, 1):
             for other in others(n):
                 plane(n, other).start()
@@ -314,32 +341,48 @@
                 plane_wait(n, other)
                 copy_c(n - 2, other).start()
 
-    def stage(t, fn):
-        @pl.when(jnp.logical_and(owner, soon if t else jnp.logical_not(soon)))
+    def stage(kind, fn):
+        this = (near, jnp.logical_and(z >= NZ // 2, zh == 0), jnp.logical_and(z < NZ // 2, zh == 1))[kind]
+
+        @pl.when(jnp.logical_and(owner, this))
         def _():
             fn()
 
+    def take_bias():
+        @pl.when(jnp.logical_not(owner))
+        def _():
+            for n in range(2):
+                for other in range(NY):
+                    local_wait(across(n, other), recv_c.at[n, other])
+
+        for n in range(NY):
+            block = bias_all[n].astype(F32).reshape(keys, channels)
+            bias_t[n] = jnp.swapaxes(block, 0, 1)[:hq]
+
+    step(2)
+    stage(0, plane_one)
+    stage(2, plane_one)
     step(3)
+    stage(0, plane_two)
     stage(1, plane_one)
+    stage(2, plane_two)
     step(4)
-    stage(0, plane_one)
     stage(1, plane_two)
     step(5)
-    stage(0, plane_two)
+    stage(0, to_core)
+    stage(2, to_core)
+    step(6)
     stage(1, to_core)
-    step(6)
-    stage(0, to_core)
+
+    @pl.when(near)
+    def _():
+        take_bias()
+
     step(7)
 
-    @pl.when(jnp.logical_not(owner))
-    def _():
-        for n in range(2):
-            for other in range(NY):
-                local_wait(across(n, other), recv_c.at[n, other])
-
-    for n in range(NY):
-        block = bias_all[n].astype(F32).reshape(keys, channels)
-        bias_t[n] = jnp.swapaxes(block, 0, 1)[:hq]
+    @pl.when(jnp.logical_not(near))
+    def _():
+        take_bias()
 
     def attend(i):
         block = gath[:, :, i].astype(F32).reshape(keys, channels).astype(BF16)
@@ -408,9 +451,13 @@
     for half in range(2):
         for far in range(2):
 
-            @pl.when(z_place(half, far) != place)
+            @pl.when(jnp.logical_and(z_place(half, far) != place, far <= zh))
             def _():
                 copy_z(half, far).wait_send()
+
+    @pl.when(giver)
+    def _():
+        copy_far().wait_send()
 
     @pl.when(owner)
     def _():
@@ -457,7 +504,8 @@
             dma((4, NY)),
             dma((2, NY)),
             dma((2, NY)),
-            pltpu.SemaphoreType.REGULAR((4, 2)),
+            dma((2,)),
+            pltpu.SemaphoreType.REGULAR,
             dma((12,)),
         ],
         compiler_params=pltpu.CompilerParams(

time: 53 us -> 47.3 us (0.89)
  Pallas kernels: 52.2 us -> 46.5 us
    pallas_call x1, Pallas kernels: 52.2 us -> 46.5 us  [local(): pl.pallas_call(functools.partial(kernel, columns), out_shape=jax.ShapeDty...]
where the time goes in v5:
time: 47.3 us; the launch traced here: 47.2 us
  Pallas kernels  46.5 us (98%)
  local copies, waits for them, and re-layouts  0.65 us (1%)
    pallas_call x1, Pallas kernels, local(): pl.pallas_call(functools.partial(kernel, columns), out_shape=jax.ShapeDty...  46.5 us

profile of v5, /device:TPU:2, one launch (start us, length us, event | category | flops | bytes accessed | tf_op | source)
XLA Modules:
  0.0 47.2 jit_solution(6445126678520449978)
XLA Ops:
  0.0 46.5 %shard_map.109 = bf16[20,24,128]{2,1,0:T(8,128)(2,1)S(1)} custom-call(bf16[48,24,128]{2,1,0:T(8,128)(2,1)} %refs_0_.1, s32[1,24]{1,0:T(1,128)} %bitcast.3, bf16[128,128]{1,0:T(8,128)(2,1)} %refs_2_.1, bf16[128,128]{1,0:T(8,128)(2,1)} %refs_3_.1, bf16[128,128]{1,0:T(8,128)(2,1)} %refs_4_.1, bf16[128,128]{1,0:T(8,128)(2,1)} %refs_5_.1, ...), custom_call_target="tpu_custom_call" | custom-call | tf_op jit(solution)/shard_map/pallas_call | solution.py:478
  46.5 0.7 %copy.13 = bf16[20,24,128]{2,1,0:T(8,128)(2,1)} copy(bf16[20,24,128]{2,1,0:T(8,128)(2,1)S(1)} %shard_map.109) | data formatting | bytes 245760

commit v6 on v5

--- a/solution.py
+++ b/solution.py
@@ -44,9 +44,9 @@
 def kernel(columns, *refs):
     inputs, out_ref, held = refs[:11], refs[11], refs[12:23]
     pair_ref, mask_ref, wq_ref, wk_ref, wv_ref, wg_ref, wb_ref, wo_ref, wha_ref, whb_ref, who_ref = held
-    gath, own, gated_ref, back, turned, bias_all, bias_t, qk_ref, mean_ref = refs[23:32]
-    send_o, send_g, recv_g, recv_p, send_r, recv_r, turn_sem, send_z, recv_z = refs[32:41]
-    send_b, recv_b, send_c, recv_c, far_sem, ready_sem, load_sem = refs[41:]
+    gath, own, gated_ref, back, turned, bias_all, bias_t, qk_ref, mean_ref, gate_ref = refs[23:33]
+    send_o, send_g, recv_g, recv_p, send_r, recv_r, turn_sem, send_z, recv_z = refs[33:42]
+    send_b, recv_b, send_c, recv_c, far_sem, ready_sem, load_sem = refs[42:]
     rows_block, _, channels = pair_ref.shape
     tokens = QR * columns
     hq = HEADS * columns
@@ -129,77 +129,14 @@
     for n in (0, 11, 6, 1, 2, 3, 4, 5, 7, 8, 9, 10):
         load(n).start()
     load(0).wait()
-    win = normalize(pair_ref[:QR].astype(F32)).astype(BF16)
-    own[...] = win.reshape(NY, GROUP, columns, channels)
+    load(11).wait()
+    normed_first = normalize(pair_ref[:columns].astype(F32))
+    own[...] = normed_first[:QR].astype(BF16).reshape(NY, GROUP, columns, channels)
     gath[y, z] = own[y]
-    greeted = (z > 0).astype(jnp.int32) + (z < NZ - 1).astype(jnp.int32) + (x != y).astype(jnp.int32)
-    greeted = greeted + getter.astype(jnp.int32)
-    greeted = greeted + 2 + 2 * zh - jnp.logical_and(owner, near).astype(jnp.int32)
-    pl.semaphore_wait(barrier, NX + NY - 1 + greeted)
-
-    def local_wait(ref, sem):
-        pltpu.make_async_copy(ref, ref, sem).wait()
-
-    def remote(src, dst, send, recv, target):
-        return pltpu.make_async_remote_copy(
-            src_ref=src, dst_ref=dst, send_sem=send, recv_sem=recv, device_id=target, device_id_type=MESH
-        )
-
-    def spread(other):
-        return remote(own.at[other], gath.at[y, z], send_o.at[other], recv_g.at[y], at_y(other))
-
-    def piece(p, zz):
-        return gath.at[pl.ds(p * JOINT, JOINT), zz]
-
-    def hop(side, p, zz):
-        target = (row, col - 1 + 2 * side)
-        return remote(piece(p, zz), piece(p, zz), send_g.at[side, p, zz], recv_p.at[p, zz], target)
-
-    def begin(p):
-        @pl.when(z < NZ - 1)
-        def _():
-            hop(1, p, z).start()
-
-        @pl.when(z > 0)
-        def _():
-            hop(0, p, z).start()
-
-    def step(t):
-        def one(o, carry):
-            p = (y // JOINT + o) % (NY // JOINT)
-
-            @pl.when(z >= t)
-            def _():
-                local_wait(piece(p, z - t), recv_p.at[p, z - t])
-
-                @pl.when(z < NZ - 1)
-                def _():
-                    hop(1, p, z - t).start()
-
-            @pl.when(z + t < NZ)
-            def _():
-                local_wait(piece(p, z + t), recv_p.at[p, z + t])
-
-                @pl.when(z > 0)
-                def _():
-                    hop(0, p, z + t).start()
-
-            return carry
-
-        lax.fori_loop(0, NY // JOINT, one, 0)
-
-    @pl.when(getter)
-    def _():
-        tell(ready_sem, at_place(z))
-
-    for d in (1, 3, 2):
-        spread((y + d) % NY).start()
-    begin(y)
-
     lane = lax.broadcasted_iota(jnp.int32, (columns, channels), 1)
     head_of = sum((lane >= columns * (h + 1)).astype(jnp.int32) for h in range(HEADS))
     lane_mod = lane - head_of * columns
-    for n in (11, 6, 1):
+    for n in (6, 1):
         load(n).wait()
     wb = wb_ref[...].astype(F32)
     wide = [jnp.broadcast_to(wb[h : h + 1], (columns, channels)) for h in range(HEADS)]
@@ -210,7 +147,7 @@
     )
     alive = jnp.sum(jnp.where(eye, mask_row, 0.0), axis=1, keepdims=True)
     for half in range(2):
-        normed = normalize(pair_ref[half * columns : (half + 1) * columns].astype(F32))
+        normed = normalize(pair_ref[columns:].astype(F32)) if half else normed_first
         full = dot_t(normed.reshape(columns * columns, channels).astype(BF16), wide)
         full = full.reshape(columns, columns, channels)
         picked = jnp.zeros((columns, channels), F32)
@@ -218,6 +155,70 @@
             picked = jnp.where(lane_mod == j, full[j], picked)
         picked = jnp.where(alive > 0.0, picked, DEAD)
         turned[0, half] = picked.astype(BF16)
+
+    greeted = (z > 0).astype(jnp.int32) + (z < NZ - 1).astype(jnp.int32) + (x != y).astype(jnp.int32)
+    greeted = greeted + getter.astype(jnp.int32)
+    greeted = greeted + 2 + 2 * zh - jnp.logical_and(owner, near).astype(jnp.int32)
+    pl.semaphore_wait(barrier, NX + NY - 1 + greeted)
+
+    def local_wait(ref, sem):
+        pltpu.make_async_copy(ref, ref, sem).wait()
+
+    def remote(src, dst, send, recv, target):
+        return pltpu.make_async_remote_copy(
+            src_ref=src, dst_ref=dst, send_sem=send, recv_sem=recv, device_id=target, device_id_type=MESH
+        )
+
+    def spread(other):
+        return remote(own.at[other], gath.at[y, z], send_o.at[other], recv_g.at[y], at_y(other))
+
+    def piece(p, zz):
+        return gath.at[pl.ds(p * JOINT, JOINT), zz]
+
+    def hop(side, p, zz):
+        target = (row, col - 1 + 2 * side)
+        return remote(piece(p, zz), piece(p, zz), send_g.at[side, p, zz], recv_p.at[p, zz], target)
+
+    def begin(p):
+        @pl.when(z < NZ - 1)
+        def _():
+            hop(1, p, z).start()
+
+        @pl.when(z > 0)
+        def _():
+            hop(0, p, z).start()
+
+    def step(t):
+        def one(o, carry):
+            p = (y + jnp.where(o > 1, 5 - o, o)) % NY
+
+            @pl.when(z >= t)
+            def _():
+                local_wait(piece(p, z - t), recv_p.at[p, z - t])
+
+                @pl.when(z < NZ - 1)
+                def _():
+                    hop(1, p, z - t).start()
+
+            @pl.when(z + t < NZ)
+            def _():
+                local_wait(piece(p, z + t), recv_p.at[p, z + t])
+
+                @pl.when(z > 0)
+                def _():
+                    hop(0, p, z + t).start()
+
+            return carry
+
+        lax.fori_loop(0, NY // JOINT, one, 0)
+
+    @pl.when(getter)
+    def _():
+        tell(ready_sem, at_place(z))
+
+    for d in (1, 3, 2):
+        spread((y + d) % NY).start()
+    begin(y)
 
     def turn():
         return remote(turned.at[0], turned.at[1], turn_sem.at[0], turn_sem.at[1], mirror)
@@ -291,9 +292,10 @@
 
     step(1)
 
-    for n in (2, 3):
+    for n in (2, 3, 5):
         load(n).wait()
     flat = gath[:, z].astype(F32).reshape(tokens, channels).astype(BF16)
+    gate_ref[...] = sigmoid(dot(flat, wg_ref[...]))
     q = (dot(flat, wq_ref[...]) * (1.0 / math.sqrt(HEAD_DIM))).astype(BF16)
     lane_t = lax.broadcasted_iota(jnp.int32, (tokens, channels), 1)
     for h in range(HEADS):
@@ -396,15 +398,14 @@
     for i in range(GROUP):
         attend(i)
 
-    for n in (4, 5, 7, 8, 9, 10):
+    for n in (4, 7, 8, 9, 10):
         load(n).wait()
     attended = jnp.zeros((tokens, channels), F32)
     for h in range(HEADS):
         mine = mean_ref[:, :, h * columns : (h + 1) * columns].reshape(tokens, channels).astype(BF16)
         inside = jnp.logical_and(lane_t >= h * HEAD_DIM, lane_t < (h + 1) * HEAD_DIM)
         attended = jnp.where(inside, dot(mine, wv_ref[...]), attended)
-    flat = gath[:, z].astype(F32).reshape(tokens, channels).astype(BF16)
-    gated = sigmoid(dot(flat, wg_ref[...])) * attended
+    gated = gate_ref[...] * attended
     gated_ref[...] = gated.reshape(NY, GROUP, columns, channels).astype(BF16)
 
     def go_home(other):
@@ -491,6 +492,7 @@
             pltpu.VMEM((NY, hq, cols * columns), F32),
             pltpu.VMEM((NY, GROUP, hq, channels), F32),
             pltpu.VMEM((NY, GROUP, hq, channels), F32),
+            pltpu.VMEM((QR * columns, channels), F32),
             dma((NY,)),
             dma((2, NY // JOINT, NZ)),
             dma((NY,)),

time: 47.3 us -> 47 us (level)
  no operation moved by 1% of the time
where the time goes in v6:
time: 47 us; the launch traced here: 46.8 us
  Pallas kernels  46.2 us (98%)
  local copies, waits for them, and re-layouts  0.65 us (1%)
    pallas_call x1, Pallas kernels, local(): pl.pallas_call(functools.partial(kernel, columns), out_shape=jax.ShapeDty...  46.2 us

profile of v6, /device:TPU:2, one launch (start us, length us, event | category | flops | bytes accessed | tf_op | source)
XLA Modules:
  0.0 46.8 jit_solution(15464032327515229269)
XLA Ops:
  0.0 46.2 %shard_map.109 = bf16[20,24,128]{2,1,0:T(8,128)(2,1)S(1)} custom-call(bf16[48,24,128]{2,1,0:T(8,128)(2,1)} %refs_0_.1, s32[1,24]{1,0:T(1,128)} %bitcast.3, bf16[128,128]{1,0:T(8,128)(2,1)} %refs_2_.1, bf16[128,128]{1,0:T(8,128)(2,1)} %refs_3_.1, bf16[128,128]{1,0:T(8,128)(2,1)} %refs_4_.1, bf16[128,128]{1,0:T(8,128)(2,1)} %refs_5_.1, ...), custom_call_target="tpu_custom_call" | custom-call | tf_op jit(solution)/shard_map/pallas_call | solution.py:479
  46.2 0.7 %copy.13 = bf16[20,24,128]{2,1,0:T(8,128)(2,1)} copy(bf16[20,24,128]{2,1,0:T(8,128)(2,1)S(1)} %shard_map.109) | data formatting | bytes 245760

commit v7 on v6

--- a/solution.py
+++ b/solution.py
@@ -400,19 +400,23 @@
 
     for n in (4, 7, 8, 9, 10):
         load(n).wait()
-    attended = jnp.zeros((tokens, channels), F32)
-    for h in range(HEADS):
-        mine = mean_ref[:, :, h * columns : (h + 1) * columns].reshape(tokens, channels).astype(BF16)
-        inside = jnp.logical_and(lane_t >= h * HEAD_DIM, lane_t < (h + 1) * HEAD_DIM)
-        attended = jnp.where(inside, dot(mine, wv_ref[...]), attended)
-    gated = gate_ref[...] * attended
-    gated_ref[...] = gated.reshape(NY, GROUP, columns, channels).astype(BF16)
+    count = GROUP * columns
+    lane_c = lax.broadcasted_iota(jnp.int32, (count, channels), 1)
 
     def go_home(other):
         return remote(gated_ref.at[other], back.at[y], send_r.at[other], recv_r.at[y], at_y(other))
 
-    for d in (1, 3, 2):
-        go_home((y + d) % NY).start()
+    for d in (2, 1, 3, 0):
+        n = (y + d) % NY
+        attended = jnp.zeros((count, channels), F32)
+        for h in range(HEADS):
+            mine = mean_ref[n, :, h * columns : (h + 1) * columns].reshape(count, channels).astype(BF16)
+            inside = jnp.logical_and(lane_c >= h * HEAD_DIM, lane_c < (h + 1) * HEAD_DIM)
+            attended = jnp.where(inside, dot(mine, wv_ref[...]), attended)
+        gated = gate_ref[pl.ds(pl.multiple_of(n * count, 8), count)] * attended
+        gated_ref[n] = gated.reshape(GROUP, columns, channels).astype(BF16)
+        if d:
+            go_home(n).start()
     back[y] = gated_ref[y]
     for d in (1, 3, 2):
         other = (y + d) % NY

time: 47 us -> 46.8 us (level)
  no operation moved by 1% of the time
where the time goes in v7:
time: 46.8 us; the launch traced here: 46.7 us
  Pallas kernels  46 us (98%)
  local copies, waits for them, and re-layouts  0.65 us (1%)
    pallas_call x1, Pallas kernels, local(): pl.pallas_call(functools.partial(kernel, columns), out_shape=jax.ShapeDty...  46 us

profile of v7, /device:TPU:2, one launch (start us, length us, event | category | flops | bytes accessed | tf_op | source)
XLA Modules:
  0.0 46.7 jit_solution(177175852016365013)
XLA Ops:
  0.0 46.0 %shard_map.109 = bf16[20,24,128]{2,1,0:T(8,128)(2,1)S(1)} custom-call(bf16[48,24,128]{2,1,0:T(8,128)(2,1)} %refs_0_.1, s32[1,24]{1,0:T(1,128)} %bitcast.3, bf16[128,128]{1,0:T(8,128)(2,1)} %refs_2_.1, bf16[128,128]{1,0:T(8,128)(2,1)} %refs_3_.1, bf16[128,128]{1,0:T(8,128)(2,1)} %refs_4_.1, bf16[128,128]{1,0:T(8,128)(2,1)} %refs_5_.1, ...), custom_call_target="tpu_custom_call" | custom-call | tf_op jit(solution)/shard_map/pallas_call | solution.py:483
  46.0 0.7 %copy.13 = bf16[20,24,128]{2,1,0:T(8,128)(2,1)} copy(bf16[20,24,128]{2,1,0:T(8,128)(2,1)S(1)} %shard_map.109) | data formatting | bytes 245760
